TPU v7x, 32 devices: a whole 2x2x4 slice. The times are simulated.
32 devices in a mesh: vec: 4 (over y, x), orb: 8 (over z, core).
Axes of the slice: x: 2, y: 2, z: 4, core: 2. Of those that a mesh axis runs over, the one named last changes fastest.
Arguments:
- chol_occ: float32 [44, 96, 1056], P('vec', 'orb'), may hold values from -6 to 6
- chol_vir: float32 [44, 960, 1056], P('vec', 'orb'), may hold values from -6 to 6
- singles: float32 [96, 960], P('orb'), may hold values from -0.6 to 0.6
Outputs:
- dressed_vir: float32 [44, 960, 1056], P('vec', 'orb')
- dressed_ov: float32 [44, 96, 960], P(None, 'orb', 'vec')
- fock_ov: float32 [96, 960], P('orb')
All inputs are finite; a program needn't handle non-finite values.
Results may differ from a plain program's by a relative error of at most 0.000086.
Values sent between devices are 32-bit elements; how exact they have to be, the bound alone decides.
A program may use at most 64 MiB of HBM per device.

v0:
```python
import jax
import jax.numpy as jnp
from jax import lax
from jax.sharding import PartitionSpec as P


def dress_right(matrix_rows, amplitudes):
    occ_width = amplitudes.shape[0]
    occ_cols = matrix_rows[:, :, :occ_width]
    extra_term = jnp.einsum("qrj,ja->qra", occ_cols, amplitudes, precision=lax.Precision.HIGHEST)
    return jnp.concatenate([occ_cols, matrix_rows[:, :, occ_width:] + extra_term], axis=2)


def dress_left(vir_rows, occ_all, amp_cols):
    return vir_rows - jnp.einsum("qin,ia->qan", occ_all, amp_cols, precision=lax.Precision.HIGHEST)


def shards(chol_occ, chol_vir, singles):
    amplitudes = lax.all_gather(singles, "orb", axis=0, tiled=True)
    occ_width = amplitudes.shape[0]
    vir_local = chol_vir.shape[1]
    vir_start = lax.axis_index("orb") * vir_local
    amp_cols = lax.dynamic_slice_in_dim(amplitudes, vir_start, vir_local, 1)
    occ_all = lax.all_gather(chol_occ, "orb", axis=1, tiled=True)
    dressed_vir = dress_right(dress_left(chol_vir, occ_all, amp_cols), amplitudes)
    dressed_occ = dress_right(chol_occ, amplitudes)
    local_rows = chol_occ.shape[1]
    first_row = lax.axis_index("orb") * local_rows
    row_ids = lax.broadcasted_iota(jnp.int32, (local_rows, chol_occ.shape[2]), 0) + first_row
    col_ids = lax.broadcasted_iota(jnp.int32, (local_rows, chol_occ.shape[2]), 1)
    diag_mask = jnp.where(row_ids == col_ids, 1.0, 0.0).astype(jnp.float32)
    traces_local = jnp.sum(chol_occ * diag_mask[None], axis=(1, 2))
    traces = lax.psum(traces_local, "orb")
    ov_block = dressed_occ[:, :, occ_width:]
    total_vectors = chol_occ.shape[0] * lax.axis_size("vec")
    fock_part = (
        jnp.einsum("q,qia->ia", traces, ov_block, precision=lax.Precision.HIGHEST) / total_vectors
    )
    fock_ov = lax.psum(fock_part, "vec")
    pair_blocks = lax.all_to_all(ov_block, "vec", split_axis=2, concat_axis=0, tiled=True)
    return (dressed_vir, pair_blocks, fock_ov)


def solution(mesh):
    return jax.shard_map(
        shards,
        mesh=mesh,
        in_specs=(P("vec", "orb", None), P("vec", "orb", None), P("orb", None)),
        out_specs=(P("vec", "orb", None), P(None, "orb", "vec"), P("orb", None)),
        check_vma=False,
    )
```

profile of v0, /device:TPU:0, one launch (start us, length us, event | category | flops | bytes accessed | tf_op | source)
XLA Modules:
  0.0 127.6 jit_solution(5254257879419233849)
XLA Ops:
  7.2 0.0 all-gather.3.cloned.1.call-start
  7.2 2.3 %copy.10 = f32[11,12,1056]{2,0,1:T(8,128)} copy(f32[11,12,1056]{2,1,0:T(8,128)} %param.3) | data formatting | bytes 1115136 | tf_op args[0]
  9.5 0.0 all-gather.3.cloned.1.call-update
  9.5 16.7 %all-gather = f32[8,12,960]{2,1,0:T(8,128)S(1)} all-gather(f32[1,12,960]{2,1,0:T(8,128)} %bitcast.22), channel_id=1, replica_groups=mesh['vec'=4,'orb'=8] {'orb'}, dimensions={0}, use_global_device_ids=true | all-gather | bytes 414720 | tf_op jit(solution)/shard_map/all_gather | solution.py:19
  26.3 1.9 %convolution_add_fusion = f32[11,12,960]{2,1,0:T(8,128)S(1)} fusion(f32[96,960,1]{1,0,2:T(8,128)S(1)} %reshape.23, f32[11,12,1056]{2,1,0:T(8,128)} %param.3), kind=kOutput, calls=%fused_computation.4 | convolution fusion | flops 146108160 | bytes 1433088 | tf_op jit(solution)/shard_map/qrj,ja->qra/dot_general | solution.py:10
  28.2 6.0 %copy.13 = f32[11,12,960]{1,0,2:T(8,128)} copy(f32[11,12,960]{2,1,0:T(8,128)S(1)} %convolution_add_fusion) | data formatting | bytes 1013760 | tf_op jit(solution)/shard_map/add | solution.py:11
  34.2 0.0 copy-start
  34.2 6.5 %reshape.27 = f32[4,1,31680]{2,1,0:T(1,128)} reshape(f32[960,11,12]{2,1,0:T(8,128)} %bitcast.20) | data formatting | bytes 1013760
  40.7 0.1 fusion.4
  40.8 0.0 copy-done
  40.8 0.2 multiply_reduce_fusion
  41.0 3.7 %all-to-all-start = ((f32[4,1,31680]{2,1,0:T(1,128)}), f32[4,1,31680]{2,1,0:T(1,128)S(1)}, u32[]{:S(2)}, u32[]{:S(2)}) async-start(f32[4,1,31680]{2,1,0:T(1,128)} %reshape.27), calls=%async_computation | async-start | bytes 1015808 | tf_op jit(solution)/shard_map/all_to_all | solution.py:40
  44.7 19.3 %psum.14 = f32[11]{0:T(128)S(1)} all-reduce(f32[11]{0:T(128)S(1)} %multiply_reduce_fusion), channel_id=1, replica_groups=mesh['vec'=4,'orb'=8] {'orb'}, use_global_device_ids=true, to_apply=%region_1.2 | all-reduce | flops 11 | bytes 88 | tf_op jit(solution)/shard_map/psum | solution.py:33
  64.0 0.8 fusion.1
  64.9 17.7 %psum.15 = f32[12,960]{1,0:T(8,128)} all-reduce(f32[12,960]{1,0:T(8,128)S(1)} %bitcast_multiply_fusion), channel_id=1, replica_groups=mesh['vec'=4,'orb'=8] {'vec'}, use_global_device_ids=true, to_apply=%region_2.3 | all-reduce | flops 11520 | bytes 92160 | tf_op jit(solution)/shard_map/psum | solution.py:39
  82.5 0.0 all-to-all-done
  82.5 0.5 broadcast.18
  83.0 2.1 %reduce = f32[4,31680]{1,0:T(4,128)S(1)} reduce(f32[4,1,31680]{2,1,0:T(1,128)S(1)} %all-to-all-done, f32[]{:T(128)} %broadcast.18), dimensions={1}, to_apply=%all_to_all.13.reduce_sub_computation | reduce | bytes 1013764 | tf_op jit(solution)/shard_map/all_to_all | solution.py:40
  85.2 6.0 %reshape.28 = f32[960,11,12]{2,1,0:T(8,128)} reshape(f32[4,31680]{1,0:T(4,128)S(1)} %reduce) | data formatting | bytes 1013760
  91.2 6.2 %copy.14 = f32[11,12,4,240]{3,0,2,1:T(8,128)S(1)} copy(f32[11,12,4,240]{1,0,3,2:T(8,128)} %bitcast.19) | data formatting | bytes 1013760 | tf_op jit(solution)/shard_map/all_to_all | solution.py:40
  97.4 0.9 all_to_all.16
  98.3 0.0 all-gather.3.cloned.1.call-done
  98.3 14.5 %bitcast_subtract_fusion = f32[11,120,1056]{1,2,0:T(8,128)S(1)} fusion(f32[11,120,1056]{1,2,0:T(8,128)} %param.4, f32[11,96,1056]{2,0,1:T(8,128)} %all-gather.3.cloned.1.call-done, f32[96,960]{1,0:T(8,128)S(1)} %reshape.21, s32[]{:T(128)S(6)} %select_n.11), kind=kOutput, calls=%fused_computation.1 | convolution fusion | flops 1607189760 | bytes 15661060 | tf_op jit(solution)/shard_map/qin,ia->qan/dot_general | solution.py:15
  112.9 4.7 %slice_add_fusion = f32[11,120,960]{1,2,0:T(8,128)S(1)} fusion(f32[11,120,1056]{1,2,0:T(8,128)S(1)} %bitcast_subtract_fusion, f32[96,960,1]{1,0,2:T(8,128)S(1)} %reshape.23), kind=kOutput, calls=%fused_computation.2 | convolution fusion | flops 1461081600 | bytes 11013120 | tf_op jit(solution)/shard_map/qrj,ja->qra/dot_general | solution.py:10
  117.6 3.2 %pad_maximum_fusion = f32[11,120,1056]{1,2,0:T(8,128)} fusion(f32[11,120,960]{1,2,0:T(8,128)S(1)} %slice_add_fusion, f32[11,120,96]{1,2,0:T(8,128)S(1)} %slice.16), kind=kLoop, calls=%fused_computation | loop fusion | flops 1393920 | bytes 11151360 | tf_op jit(solution)/shard_map/concatenate | solution.py:11
  (5 shorter events, 0.1 us)
Async XLA Ops:
  7.2 91.1 %all-gather.3.cloned.1.call-start = ((), (), s32[]{:S(2)}) async-start(), calls=%async_computation.1 | async-start | bytes 7962624 | tf_op jit(solution)/shard_map/all_gather | solution.py:24
  34.2 6.6 %copy-start = (f32[11,12,1056]{2,1,0:T(8,128)S(1)}, f32[11,12,1056]{2,1,0:T(8,128)}, u32[]{:S(2)}) copy-start(f32[11,12,1056]{2,1,0:T(8,128)} %param.3) | copy-start | bytes 1672708
  41.0 41.6 %all-to-all-start = ((f32[4,1,31680]{2,1,0:T(1,128)}), f32[4,1,31680]{2,1,0:T(1,128)S(1)}, u32[]{:S(2)}, u32[]{:S(2)}) async-start(f32[4,1,31680]{2,1,0:T(1,128)} %reshape.27), calls=%async_computation | async-start | bytes 1015808 | tf_op jit(solution)/shard_map/all_to_all | solution.py:40
Sparse Core Ops, SparseCore 0:
  10.2 74.4 all-gather.2
where the time goes:
time: 128 us
  blocking collectives  53.7 us (42%)
  local copies, waits for them, and re-layouts  28.5 us (22%)
  matrix products  22 us (17%)
  between operations  14.1 us (11%)
  other arithmetic  5.58 us (4%)
  starting transfers between devices  3.76 us (3%)
    psum x1, blocking collectives, shards(): traces = lax.psum(traces_local, 'orb')  19.3 us
    psum x1, blocking collectives, shards(): fock_ov = lax.psum(fock_part, 'vec')  17.7 us
    all_gather x1, blocking collectives, shards(): amplitudes = lax.all_gather(singles, 'orb', axis=0, tiled=True)  16.7 us
    unnamed x7, local copies, waits for them, and re-layouts  14.9 us
    dot_general x1, matrix products, dress_left(): jnp.einsum('qin,ia->qan', occ_all, amp_cols, precision=lax.Precision.HIGH...  14.5 us
    all_to_all x3, local copies, waits for them, and re-layouts, shards(): lax.all_to_all(ov_block, 'vec', split_axis=2, concat_axis=0, tiled=True)  7.57 us
    dot_general x2, matrix products, dress_right(): jnp.einsum('qrj,ja->qra', occ_cols, amplitudes, precision=lax.Precision.H...  6.66 us
    add x1, local copies, waits for them, and re-layouts, dress_right(): matrix_rows[:, :, occ_width:] + extra_term  5.96 us
  transfers between devices with their start and end apart: 2, of which 0 were waited for; matrix products, arithmetic and copies ran while one was open for 24% of the time, Pallas kernels for 0%

commit v1 on v0

--- a/solution.py
+++ b/solution.py
@@ -2,6 +2,28 @@
 import jax.numpy as jnp
 from jax import lax
 from jax.sharding import PartitionSpec as P
+
+
+def joined_along(tiles, dim):
+    tiles = jnp.moveaxis(tiles, 0, dim)
+    shape = tiles.shape
+    return tiles.reshape(*shape[:dim], shape[dim] * shape[dim + 1], *shape[dim + 2 :])
+
+
+def collected_by_bits(x, axis):
+    size = lax.axis_size(axis)
+    tiles = x[None]
+    for level in range(size.bit_length() - 1):
+        stride = 1 << level
+        theirs = lax.ppermute(tiles, axis, [(i, i ^ stride) for i in range(size)])
+        both = jnp.stack([tiles, theirs])
+        upper = lax.axis_index(axis) >> level & 1
+        tiles = jnp.where(upper == 0, both, both[::-1]).reshape(-1, *x.shape)
+    return tiles
+
+
+def collect(array, axis, dim):
+    return joined_along(collected_by_bits(array, axis), dim)
 
 
 def dress_right(matrix_rows, amplitudes):
@@ -16,7 +38,7 @@
 
 
 def shards(chol_occ, chol_vir, singles):
-    amplitudes = lax.all_gather(singles, "orb", axis=0, tiled=True)
+    amplitudes = collect(singles, "orb", 0)
     occ_width = amplitudes.shape[0]
     vir_local = chol_vir.shape[1]
     vir_start = lax.axis_index("orb") * vir_local

time: 128 us -> 142 us (1.11)
  the two profiles are of different devices: /device:TPU:0 before, /device:TPU:16 now
where the time goes in v1:
time: 142 us
  blocking collectives  58.3 us (41%)
  local copies, waits for them, and re-layouts  28.4 us (20%)
  matrix products  22 us (15%)
  between operations  14.2 us (10%)
  other arithmetic  7.79 us (5%)
  starting transfers between devices  5.58 us (4%)
  waiting for transfers between devices  5.44 us (4%)
    psum x1, blocking collectives, shards(): traces = lax.psum(traces_local, 'orb')  40.3 us
    psum x1, blocking collectives, shards(): fock_ov = lax.psum(fock_part, 'vec')  18 us
    unnamed x3, local copies, waits for them, and re-layouts  14.7 us
    dot_general x1, matrix products, dress_left(): jnp.einsum('qin,ia->qan', occ_all, amp_cols, precision=lax.Precision.HIGH...  14.5 us
    all_to_all x3, local copies, waits for them, and re-layouts, shards(): lax.all_to_all(ov_block, 'vec', split_axis=2, concat_axis=0, tiled=True)  7.57 us
    dot_general x2, matrix products, dress_right(): jnp.einsum('qrj,ja->qra', occ_cols, amplitudes, precision=lax.Precision.H...  6.69 us
    add x1, local copies, waits for them, and re-layouts, dress_right(): matrix_rows[:, :, occ_width:] + extra_term  5.96 us
    ppermute x3, waiting for transfers between devices, collected_by_bits(): theirs = lax.ppermute(tiles, axis, [(i, i ^ stride) for i in range(size)])  5.42 us
  transfers between devices with their start and end apart: 5, of which 2 were waited for; matrix products, arithmetic and copies ran while one was open for 23% of the time, Pallas kernels for 0%

profile of v1, /device:TPU:16, one launch (start us, length us, event | category | flops | bytes accessed | tf_op | source)
XLA Modules:
  0.0 141.7 jit_solution(13422900668998691190)
XLA Ops:
  7.2 0.0 all-gather.2.cloned.1.call-start
  7.2 2.3 %copy.10 = f32[11,12,1056]{2,0,1:T(8,128)} copy(f32[11,12,1056]{2,1,0:T(8,128)} %param.3) | data formatting | bytes 1115136 | tf_op args[0]
  9.5 0.0 all-gather.2.cloned.1.call-update
  9.5 0.1 collective-permute-start
  9.6 1.4 %collective-permute-done = f32[1,12,960]{2,1,0:T(8,128)S(1)} collective-permute-done((f32[1,12,960]{2,1,0:T(8,128)}, f32[1,12,960]{2,1,0:T(8,128)S(1)}, u32[]{:S(2)}, u32[]{:S(2)}) %collective-permute-start) | collective-permute-done | bytes 46112 | tf_op jit(solution)/shard_map/ppermute | solution.py:18
  11.0 0.8 pad_maximum_fusion.3
  11.9 1.6 %collective-permute-start.1 = (f32[2,12,960]{2,1,0:T(8,128)S(1)}, f32[2,12,960]{2,1,0:T(8,128)S(1)}, u32[]{:S(2)}, u32[]{:S(2)}) collective-permute-start(f32[2,12,960]{2,1,0:T(8,128)S(1)} %get-tuple-element.4), channel_id=1, source_target_pairs={{0,2},{1,3},{2,0},{3,1},{4,6},{5,7},{6,4},{7,5},{8,10},{9,11},{10,... | collective-permute-start | bytes 276488 | tf_op jit(solution)/shard_map/ppermute | solution.py:18
  13.6 4.0 %collective-permute-done.1 = f32[2,12,960]{2,1,0:T(8,128)S(1)} collective-permute-done((f32[2,12,960]{2,1,0:T(8,128)S(1)}, f32[2,12,960]{2,1,0:T(8,128)S(1)}, u32[]{:S(2)}, u32[]{:S(2)}) %collective-permute-start.1) | collective-permute-done | bytes 92192 | tf_op jit(solution)/shard_map/ppermute | solution.py:18
  17.6 0.2 collective-permute-start.2
  17.8 0.1 fusion.7
  17.9 1.4 multiply_reduce_fusion
  19.3 40.3 %psum.14 = f32[11]{0:T(128)S(1)} all-reduce(f32[11]{0:T(128)S(1)} %multiply_reduce_fusion), channel_id=1, replica_groups=mesh['vec'=4,'orb'=8] {'orb'}, use_global_device_ids=true, to_apply=%region_1.2 | all-reduce | flops 11 | bytes 88 | tf_op jit(solution)/shard_map/psum | solution.py:55
  59.6 0.0 collective-permute-done.2
  59.8 2.0 %fusion.1 = f32[11,12,960]{2,1,0:T(8,128)S(1)} fusion(f32[96,960,1]{1,0,2:T(8,128)S(1)} %reshape.29, f32[11,12,1056]{2,1,0:T(8,128)} %param.3), kind=kOutput, calls=%fused_computation.5 | convolution fusion | flops 146108160 | bytes 1433088 | tf_op jit(solution)/shard_map/qrj,ja->qra/dot_general | solution.py:32
  61.8 6.0 %copy.13 = f32[11,12,960]{1,0,2:T(8,128)} copy(f32[11,12,960]{2,1,0:T(8,128)S(1)} %fusion.1) | data formatting | bytes 1013760 | tf_op jit(solution)/shard_map/add | solution.py:33
  67.7 6.4 %reshape.33 = f32[4,1,31680]{2,1,0:T(1,128)} reshape(f32[960,11,12]{2,1,0:T(8,128)} %bitcast.34) | data formatting | bytes 1013760
  74.1 3.6 %all-to-all-start = ((f32[4,1,31680]{2,1,0:T(1,128)}), f32[4,1,31680]{2,1,0:T(1,128)S(1)}, u32[]{:S(2)}, u32[]{:S(2)}) async-start(f32[4,1,31680]{2,1,0:T(1,128)} %reshape.33), calls=%async_computation | async-start | bytes 1015808 | tf_op jit(solution)/shard_map/all_to_all | solution.py:62
  77.7 0.8 fusion.2
  78.6 18.0 %psum.15 = f32[12,960]{1,0:T(8,128)} all-reduce(f32[12,960]{1,0:T(8,128)S(1)} %bitcast_multiply_fusion), channel_id=1, replica_groups=mesh['vec'=4,'orb'=8] {'vec'}, use_global_device_ids=true, to_apply=%region_2.3 | all-reduce | flops 11520 | bytes 92160 | tf_op jit(solution)/shard_map/psum | solution.py:61
  96.6 0.0 all-to-all-done
  96.6 0.5 broadcast.18
  97.1 2.1 %reduce = f32[4,31680]{1,0:T(4,128)S(1)} reduce(f32[4,1,31680]{2,1,0:T(1,128)S(1)} %all-to-all-done, f32[]{:T(128)} %broadcast.18), dimensions={1}, to_apply=%all_to_all.13.reduce_sub_computation | reduce | bytes 1013764 | tf_op jit(solution)/shard_map/all_to_all | solution.py:62
  99.2 6.0 %reshape.34 = f32[960,11,12]{2,1,0:T(8,128)} reshape(f32[4,31680]{1,0:T(4,128)S(1)} %reduce) | data formatting | bytes 1013760
  105.3 6.2 %copy.14 = f32[11,12,4,240]{3,0,2,1:T(8,128)S(1)} copy(f32[11,12,4,240]{1,0,3,2:T(8,128)} %bitcast.33) | data formatting | bytes 1013760 | tf_op jit(solution)/shard_map/all_to_all | solution.py:62
  111.4 0.9 all_to_all.16
  112.3 0.0 all-gather.2.cloned.1.call-done
  112.3 14.5 %bitcast_subtract_fusion = f32[11,120,1056]{1,2,0:T(8,128)S(1)} fusion(f32[11,120,1056]{1,2,0:T(8,128)} %param.4, f32[11,96,1056]{2,0,1:T(8,128)} %all-gather.2.cloned.1.call-done, f32[96,960]{1,0:T(8,128)S(1)} %reshape_reshape.3, s32[]{:T(128)S(6)} %select_n.41), kind=kOutput, calls=%fused_computation.1 | convolution fusion | flops 1607189760 | bytes 15661060 | tf_op jit(solution)/shard_map/qin,ia->qan/dot_general | solution.py:37
  126.9 4.7 %slice_add_fusion = f32[11,120,960]{1,2,0:T(8,128)S(1)} fusion(f32[11,120,1056]{1,2,0:T(8,128)S(1)} %bitcast_subtract_fusion, f32[96,960,1]{1,0,2:T(8,128)S(1)} %reshape.29), kind=kOutput, calls=%fused_computation.2 | convolution fusion | flops 1461081600 | bytes 11013120 | tf_op jit(solution)/shard_map/qrj,ja->qra/dot_general | solution.py:32
  131.7 3.2 %pad_maximum_fusion = f32[11,120,1056]{1,2,0:T(8,128)} fusion(f32[11,120,960]{1,2,0:T(8,128)S(1)} %slice_add_fusion, f32[11,120,96]{1,2,0:T(8,128)S(1)} %slice.16), kind=kLoop, calls=%fused_computation | loop fusion | flops 1393920 | bytes 11151360 | tf_op jit(solution)/shard_map/concatenate | solution.py:33
  (10 shorter events, 0.3 us)
Async XLA Ops:
  7.2 105.2 %all-gather.2.cloned.1.call-start = ((), (), s32[]{:S(2)}) async-start(), calls=%async_computation.1 | async-start | bytes 7962624 | tf_op jit(solution)/shard_map/all_gather | solution.py:46
  9.5 1.5 %collective-permute-start = (f32[1,12,960]{2,1,0:T(8,128)}, f32[1,12,960]{2,1,0:T(8,128)S(1)}, u32[]{:S(2)}, u32[]{:S(2)}) collective-permute-start(f32[1,12,960]{2,1,0:T(8,128)} %bitcast.40), channel_id=1, source_target_pairs={{0,1},{1,0},{2,3},{3,2},{4,5},{5,4},{6,7},{7,6},{8,9},{9,8},{10,11... | collective-permute-start | bytes 138248 | tf_op jit(solution)/shard_map/ppermute | solution.py:18
  11.9 5.6 %collective-permute-start.1 = (f32[2,12,960]{2,1,0:T(8,128)S(1)}, f32[2,12,960]{2,1,0:T(8,128)S(1)}, u32[]{:S(2)}, u32[]{:S(2)}) collective-permute-start(f32[2,12,960]{2,1,0:T(8,128)S(1)} %get-tuple-element.4), channel_id=1, source_target_pairs={{0,2},{1,3},{2,0},{3,1},{4,6},{5,7},{6,4},{7,5},{8,10},{9,11},{10,... | collective-permute-start | bytes 276488 | tf_op jit(solution)/shard_map/ppermute | solution.py:18
  17.6 42.0 %collective-permute-start.2 = (f32[4,12,960]{2,1,0:T(8,128)S(1)}, f32[4,12,960]{2,1,0:T(8,128)S(1)}, u32[]{:S(2)}, u32[]{:S(2)}) collective-permute-start(f32[4,12,960]{2,1,0:T(8,128)S(1)} %bitcast.36), channel_id=1, source_target_pairs={{0,4},{1,5},{2,6},{3,7},{4,0},{5,1},{6,2},{7,3},{8,12},{9,13},{10,... | collective-permute-start | bytes 552968 | tf_op jit(solution)/shard_map/ppermute | solution.py:18
  74.1 22.4 %all-to-all-start = ((f32[4,1,31680]{2,1,0:T(1,128)}), f32[4,1,31680]{2,1,0:T(1,128)S(1)}, u32[]{:S(2)}, u32[]{:S(2)}) async-start(f32[4,1,31680]{2,1,0:T(1,128)} %reshape.33), calls=%async_computation | async-start | bytes 1015808 | tf_op jit(solution)/shard_map/all_to_all | solution.py:62
Sparse Core Ops, SparseCore 0:
  10.2 76.0 all-gather.1
